TPU v7x, 32 devices: a whole 2x2x4 slice. The times are simulated.
32 devices in a mesh: row: 2 (over y), col: 8 (over z, x), depth: 2 (over core).
Axes of the slice: x: 2, y: 2, z: 4, core: 2. Of those that a mesh axis runs over, the one named last changes fastest.
Arguments:
- a_tiles: bfloat16 [2, 16, 8, 2, 128, 128], P('row', ('col', 'depth')), may hold values from -1.5 to 1.5
- a_cols: int32 [2, 16, 8, 2], P('row', ('col', 'depth')), may hold values from 0 to 15, as said below
- a_count: int32 [2, 16, 8], P('row', ('col', 'depth')), may hold values from 0 to 2, as said below
- b_tiles: bfloat16 [4, 2, 2, 8, 16, 1, 128, 128], P(None, 'row', 'depth', 'col'), may hold values from -1.5 to 1.5
- b_cols: int32 [4, 2, 2, 8, 16, 1], P(None, 'row', 'depth', 'col'), may hold values from 0 to 11, as said below
- b_count: int32 [4, 2, 2, 8, 16], P(None, 'row', 'depth', 'col'), may hold values from 0 to 1, as said below
Outputs:
- product: bfloat16 [2048, 12288], P(('row', 'depth'), 'col')
Inputs may be any that keep to these rules, and one draw needn't show every extreme that they name: The entries of a_cols for one row group, inner panel and block row are distinct. `a_count`: some block row holds 2 blocks in every draw. The entries of b_cols for one inner block row are distinct. `b_count`: some inner block row holds 1 block in every draw.
All inputs are finite; a program needn't handle non-finite values.
Results may differ from a plain program's by a relative error of at most 0.001.
Values may be sent and summed in bfloat16 or wider, within the bound.
A program may use at most 128 MiB of HBM per device.

v0:
```python
import math
import jax
import jax.numpy as jnp
from jax import lax
from jax.sharding import PartitionSpec as P

BC = 12
SHIFTS = 4


def for_sending(array):
    return jax.tree.map(lambda a: a.astype(jnp.bfloat16) if a.dtype == jnp.float32 else a, array)


def shifted(value, axis, steps):
    count = lax.axis_size(axis)
    pairs = [(source, (source + steps) % count) for source in range(count)]
    return lax.ppermute(value, axis, pairs)


def dense_panel(tiles_b, cols_b, count_b, width):
    slot_ids = lax.broadcasted_iota(jnp.int32, cols_b.shape, 1)
    valid_slot = slot_ids < count_b[:, None]
    targets = lax.broadcasted_iota(jnp.int32, (1, 1, width), 2)
    placing = jnp.logical_and(cols_b[:, :, None] == targets, valid_slot[:, :, None]).astype(
        jnp.bfloat16
    )
    spread = jnp.einsum("kuc,kuab->kacb", placing, tiles_b, preferred_element_type=jnp.float32)
    inner_blocks = tiles_b.shape[0]
    tile_size = tiles_b.shape[2]
    return spread.astype(jnp.bfloat16).reshape(inner_blocks, tile_size, width * tile_size)


def panel_product(tiles_a, cols_a, count_a, rows_dense):
    block_rows = tiles_a.shape[0]
    per_row = tiles_a.shape[1]
    tile_size = tiles_a.shape[2]
    slot_ids = lax.broadcasted_iota(jnp.int32, cols_a.shape, 1)
    valid_slot = slot_ids < count_a[:, None]
    masked = jnp.where(valid_slot[:, :, None, None], tiles_a, jnp.zeros_like(tiles_a))
    group_rows = math.gcd(block_rows, 4)

    def one_group(pieces):
        tiles_part, cols_part = pieces
        chosen = jnp.take(rows_dense, cols_part, axis=0)
        return jnp.einsum("rtab,rtbn->ran", tiles_part, chosen, preferred_element_type=jnp.float32)

    grouped = lax.map(
        one_group,
        (
            masked.reshape(block_rows // group_rows, group_rows, per_row, tile_size, tile_size),
            cols_a.reshape(block_rows // group_rows, group_rows, per_row),
        ),
    )
    return grouped.reshape(block_rows, tile_size, rows_dense.shape[2])


def roll_slots(stack, offset):
    slot_total = stack[0].shape[0]
    return tuple(
        (
            lax.dynamic_slice_in_dim(
                jnp.concatenate([member, member], 0), offset % slot_total, slot_total, 0
            )
            for member in stack
        )
    )


def select_if(flag, fresh, stale):
    return tuple((jnp.where(flag, new_part, old_part) for new_part, old_part in zip(fresh, stale)))


def local(a_tiles, a_cols, a_count, b_tiles, b_cols, b_count):
    rows_axis = lax.axis_size("row")
    cols_axis = lax.axis_size("col")
    row_group = lax.axis_index("row")
    col_group = lax.axis_index("col")
    tiles_a = a_tiles[0, 0]
    cols_a = a_cols[0, 0]
    count_a = a_count[0, 0]
    tiles_b = b_tiles[:, 0, 0, 0]
    cols_b = b_cols[:, 0, 0, 0]
    count_b = b_count[:, 0, 0, 0]
    for bit_pos in range((rows_axis - 1).bit_length()):
        stride = 1 << bit_pos
        moved = (
            shifted(tiles_a, "col", cols_axis - stride),
            shifted(for_sending(cols_a), "col", cols_axis - stride).astype(cols_a.dtype),
            shifted(for_sending(count_a), "col", cols_axis - stride).astype(count_a.dtype),
        )
        tiles_a, cols_a, count_a = select_if(
            row_group // stride % 2 == 1, moved, (tiles_a, cols_a, count_a)
        )
    for bit_pos in range((cols_axis - 1).bit_length()):
        stride = 1 << bit_pos
        nearby = stride % rows_axis
        if nearby:
            moved = (
                shifted(tiles_b, "row", rows_axis - nearby),
                shifted(for_sending(cols_b), "row", rows_axis - nearby).astype(cols_b.dtype),
                shifted(for_sending(count_b), "row", rows_axis - nearby).astype(count_b.dtype),
            )
        else:
            moved = (tiles_b, cols_b, count_b)
        moved = roll_slots(moved, (row_group + stride) // rows_axis)
        tiles_b, cols_b, count_b = select_if(
            col_group // stride % 2 == 1, moved, (tiles_b, cols_b, count_b)
        )
    tile_size = tiles_a.shape[2]
    running = jnp.zeros((tiles_a.shape[0], tile_size, BC * tile_size), jnp.float32)
    for turn_no in range(SHIFTS):
        current_tiles = tiles_b[0]
        current_cols = cols_b[0]
        current_count = count_b[0]
        rows_dense = dense_panel(current_tiles, current_cols, current_count, BC)
        running = running + panel_product(tiles_a, cols_a, count_a, rows_dense)
        if turn_no + 1 < SHIFTS:
            tiles_a, cols_a, count_a = (
                shifted(tiles_a, "col", cols_axis - 1),
                shifted(for_sending(cols_a), "col", cols_axis - 1).astype(cols_a.dtype),
                shifted(for_sending(count_a), "col", cols_axis - 1).astype(count_a.dtype),
            )
            moved = (
                shifted(tiles_b, "row", rows_axis - 1),
                shifted(for_sending(cols_b), "row", rows_axis - 1).astype(cols_b.dtype),
                shifted(for_sending(count_b), "row", rows_axis - 1).astype(count_b.dtype),
            )
            tiles_b, cols_b, count_b = roll_slots(moved, (row_group + 1) // rows_axis)
    flat_running = running.reshape(-1, running.shape[2])
    summed = lax.psum(flat_running, "depth")
    half_rows = flat_running.shape[0] // lax.axis_size("depth")
    own_rows = lax.dynamic_slice_in_dim(summed, lax.axis_index("depth") * half_rows, half_rows, 0)
    return own_rows.astype(jnp.bfloat16)


def solution(mesh):
    placed = (
        P("row", ("col", "depth"), None, None, None, None),
        P("row", ("col", "depth"), None, None),
        P("row", ("col", "depth"), None),
        P(None, "row", "depth", "col", None, None, None, None),
        P(None, "row", "depth", "col", None, None),
        P(None, "row", "depth", "col", None),
    )
    return jax.shard_map(
        local, mesh=mesh, in_specs=placed, out_specs=P(("row", "depth"), "col"), check_vma=False
    )
```

profile of v0, /device:TPU:0, one launch (start us, length us, event | category | flops | bytes accessed | tf_op | source)
XLA Modules:
  0.0 308.4 jit_solution(8262394096898452640)
XLA Ops:
  0.0 6.1 %collective-permute-start = (s32[8]{0:T(128)}, s32[8]{0:T(128)S(1)}, u32[]{:S(2)}, u32[]{:S(2)}) collective-permute-start(s32[8]{0:T(128)} %bitcast.190), channel_id=1, source_target_pairs={{0,14},{2,0},{4,2},{6,4},{8,6},{10,8},{12,10},{14,12},{1,15},{3,1}... | collective-permute-start | bytes 104 | tf_op jit(solution)/shard_map/ppermute | solution.py:18
  15.4 6.1 %collective-permute-done.6 = s32[8]{0:T(128)S(1)} collective-permute-done((s32[8]{0:T(128)S(1)}, s32[8]{0:T(128)S(1)}, u32[]{:S(2)}, u32[]{:S(2)}) %collective-permute-start.6) | collective-permute-done | bytes 64 | tf_op jit(solution)/shard_map/ppermute | solution.py:18
  21.6 4.1 %collective-permute-start.12 = (s32[8]{0:T(128)S(1)}, s32[8]{0:T(128)S(1)}, u32[]{:S(2)}, u32[]{:S(2)}) collective-permute-start(s32[8]{0:T(128)S(1)} %collective-permute-done.6), channel_id=1, source_target_pairs={{0,14},{2,0},{4,2},{6,4},{8,6},{10,8},{12,10},{14,12},{1,15},{3,1}... | collective-permute-start | bytes 104 | tf_op jit(solution)/shard_map/ppermute | solution.py:18
  27.0 5.0 %collective-permute-start.18 = (s32[8]{0:T(128)S(1)}, s32[8]{0:T(128)S(1)}, u32[]{:S(2)}, u32[]{:S(2)}) collective-permute-start(s32[8]{0:T(128)S(1)} %collective-permute-done.12), channel_id=1, source_target_pairs={{0,14},{2,0},{4,2},{6,4},{8,6},{10,8},{12,10},{14,12},{1,15},{3,1}... | collective-permute-start | bytes 104 | tf_op jit(solution)/shard_map/ppermute | solution.py:18
  33.3 5.0 %collective-permute-start.8 = (s32[8,2]{0,1:T(2,128)S(1)}, s32[8,2]{0,1:T(2,128)S(1)}, u32[]{:S(2)}, u32[]{:S(2)}) collective-permute-start(s32[8,2]{0,1:T(2,128)S(1)} %broadcast_select_fusion.5), channel_id=1, source_target_pairs={{0,14},{2,0},{4,2},{6,4},{8,6},{10,8},{12,10},{14,12},{1,15},{3,1}... | collective-permute-start | bytes 200 | tf_op jit(solution)/shard_map/ppermute | solution.py:18
  39.6 5.0 %collective-permute-start.14 = (s32[8,2]{0,1:T(2,128)S(1)}, s32[8,2]{0,1:T(2,128)S(1)}, u32[]{:S(2)}, u32[]{:S(2)}) collective-permute-start(s32[8,2]{0,1:T(2,128)S(1)} %collective-permute-done.8), channel_id=1, source_target_pairs={{0,14},{2,0},{4,2},{6,4},{8,6},{10,8},{12,10},{14,12},{1,15},{3,1}... | collective-permute-start | bytes 200 | tf_op jit(solution)/shard_map/ppermute | solution.py:18
  45.9 5.0 %collective-permute-start.20 = (s32[8,2]{0,1:T(2,128)S(1)}, s32[8,2]{0,1:T(2,128)S(1)}, u32[]{:S(2)}, u32[]{:S(2)}) collective-permute-start(s32[8,2]{0,1:T(2,128)S(1)} %collective-permute-done.14), channel_id=1, source_target_pairs={{0,14},{2,0},{4,2},{6,4},{8,6},{10,8},{12,10},{14,12},{1,15},{3,1}... | collective-permute-start | bytes 200 | tf_op jit(solution)/shard_map/ppermute | solution.py:18
  53.4 5.9 %collective-permute-done.10 = s32[4,16,1]{1,0,2:T(4,128)S(1)} collective-permute-done((s32[4,16,1]{1,0,2:T(4,128)S(1)}, s32[4,16,1]{1,0,2:T(4,128)S(1)}, u32[]{:S(2)}, u32[]{:S(2)}) %collective-permute-start.10) | collective-permute-done | bytes 288 | tf_op jit(solution)/shard_map/ppermute | solution.py:18
  68.3 11.7 %collective-permute-done.7 = bf16[8,2,128,128]{3,2,1,0:T(8,128)(2,1)S(1)} collective-permute-done((bf16[8,2,128,128]{3,2,1,0:T(8,128)(2,1)S(1)}, bf16[8,2,128,128]{3,2,1,0:T(8,128)(2,1)S(1)}, u32[]{:S(2)}, u32[]{:S(2)}) %collective-permute-start.7) | collective-permute-done | bytes 524320 | tf_op jit(solution)/shard_map/ppermute | solution.py:18
  81.6 12.1 %collective-permute-done.13 = bf16[8,2,128,128]{3,2,1,0:T(8,128)(2,1)S(1)} collective-permute-done((bf16[8,2,128,128]{3,2,1,0:T(8,128)(2,1)S(1)}, bf16[8,2,128,128]{3,2,1,0:T(8,128)(2,1)S(1)}, u32[]{:S(2)}, u32[]{:S(2)}) %collective-permute-start.13) | collective-permute-done | bytes 524320 | tf_op jit(solution)/shard_map/ppermute | solution.py:18
  105.1 3.4 %broadcast.166.clone.2 = f32[2,4,128,1536]{3,2,1,0:T(8,128)} broadcast(f32[]{:T(128)} %constant.191.clone.1), dimensions={} | broadcast | bytes 6291460 | tf_op jit(solution)/shard_map/broadcast.11
  108.5 34.5 %while.44 = (s32[]{:T(128)}, f32[2,4,128,1536]{3,2,1,0:T(8,128)}, bf16[2,4,2,128,128]{4,3,2,1,0:T(8,128)(2,1)}, s32[2,4,2]{1,0,2:T(2,128)S(1)}, f32[16,12]{1,0:T(8,128)S(1)}, /*index=5*/f32[16,128,128]{1,2,0:T(8,128)}, s32[]{:T(128)}) while((s32[]{:T(128)}, f32[2,4,128,1536]{3,2,1,0:T(8,128)}, ...), condition=%wide.region_1.3_spmd.clone, body=%wide.region_0.2_spmd.clone.sunk | while | flops 410518592 | bytes 26482904 | solution.py:48
  108.8 5.0 %multiply_convert_fusion.8 = bf16[16,128,128,12]{1,2,3,0:T(8,128)(2,1)} fusion(f32[16,12]{1,0:T(8,128)S(1)} %get-tuple-element.488, f32[16,128,128]{1,2,0:T(8,128)} %get-tuple-element.489), kind=kLoop, calls=%fused_computation.8.clone.1 | loop fusion | flops 6291456 | bytes 7340800 | tf_op jit(solution)/shard_map/convert_element_type | solution.py:31
  113.8 5.4 %gather_fusion = bf16[8,128,1536]{1,2,0:T(8,128)(2,1)} fusion(bf16[16,128,1536]{1,2,0:T(8,128)(2,1)} %bitcast.162, s32[1024]{0:T(1024)S(1)} %pad_clamp_fusion.8), kind=kCustom, calls=%fused_computation.clone.clone.1 | custom fusion | bytes 6291488 | tf_op jit(solution)/shard_map/while/body/eval_jaxpr/jit(_take)/gather | solution.py:45
  119.2 3.2 %copy.57 = bf16[4,2,128,1536]{3,2,1,0:T(8,128)(2,1)S(1)} copy(bf16[4,2,128,1536]{2,3,1,0:T(8,128)(2,1)} %bitcast.166) | data formatting | bytes 6291456 | tf_op jit(solution)/shard_map/while/body/eval_jaxpr/jit(_take)/gather | solution.py:45
  122.4 3.4 %fusion.80 = f32[2,4,128,1536]{3,2,1,0:T(8,128)} fusion(f32[2,4,128,1536]{3,2,1,0:T(8,128)} %get-tuple-element.478, s32[]{:T(128)S(6)} %copy.86, bf16[4,2,128,1536]{3,2,1,0:T(8,128)(2,1)S(1)} %copy.57, pred[4,2]{1,0:T(4,128)(4,1)S(1)} %copy.58, bf16[2,4,2,128,128]{4,3,2,1,0:T(8,128)(2,1)} %get-tuple-element.486), kind=kOutput, calls=%fused_computation.10.clone.1 | convolution fusion | flops 404226048 | bytes 6554632 | tf_op jit(solution)/shard_map/while/body/eval_jaxpr/rtab,rtbn->ran/dot_general | solution.py:46
  126.1 5.0 %multiply_convert_fusion.8 = bf16[16,128,128,12]{1,2,3,0:T(8,128)(2,1)} fusion(f32[16,12]{1,0:T(8,128)S(1)} %get-tuple-element.488, f32[16,128,128]{1,2,0:T(8,128)} %get-tuple-element.489), kind=kLoop, calls=%fused_computation.8.clone.1 | loop fusion | flops 6291456 | bytes 7340800 | tf_op jit(solution)/shard_map/convert_element_type | solution.py:31
  131.0 5.4 %gather_fusion = bf16[8,128,1536]{1,2,0:T(8,128)(2,1)} fusion(bf16[16,128,1536]{1,2,0:T(8,128)(2,1)} %bitcast.162, s32[1024]{0:T(1024)S(1)} %pad_clamp_fusion.8), kind=kCustom, calls=%fused_computation.clone.clone.1 | custom fusion | bytes 6291488 | tf_op jit(solution)/shard_map/while/body/eval_jaxpr/jit(_take)/gather | solution.py:45
  136.5 3.2 %copy.57 = bf16[4,2,128,1536]{3,2,1,0:T(8,128)(2,1)S(1)} copy(bf16[4,2,128,1536]{2,3,1,0:T(8,128)(2,1)} %bitcast.166) | data formatting | bytes 6291456 | tf_op jit(solution)/shard_map/while/body/eval_jaxpr/jit(_take)/gather | solution.py:45
  139.7 3.4 %fusion.80 = f32[2,4,128,1536]{3,2,1,0:T(8,128)} fusion(f32[2,4,128,1536]{3,2,1,0:T(8,128)} %get-tuple-element.478, s32[]{:T(128)S(6)} %copy.86, bf16[4,2,128,1536]{3,2,1,0:T(8,128)(2,1)S(1)} %copy.57, pred[4,2]{1,0:T(4,128)(4,1)S(1)} %copy.58, bf16[2,4,2,128,128]{4,3,2,1,0:T(8,128)(2,1)} %get-tuple-element.486), kind=kOutput, calls=%fused_computation.10.clone.1 | convolution fusion | flops 404226048 | bytes 6554632 | tf_op jit(solution)/shard_map/while/body/eval_jaxpr/rtab,rtbn->ran/dot_general | solution.py:46
  143.0 3.7 %fusion.41 = bf16[4,16,1,128,128]{3,4,1,2,0:T(8,128)(2,1)} fusion(s32[]{:T(128)S(6)} %select_n.231, bf16[4,16,1,128,128]{3,4,1,2,0:T(8,128)(2,1)} %collective-permute-done.9), kind=kLoop, calls=%fused_computation.79 | loop fusion | flops 1048576 | bytes 4194308 | tf_op jit(solution)/shard_map/concatenate | solution.py:63
  149.4 3.5 %broadcast.166.clone.3 = f32[2,4,128,1536]{3,2,1,0:T(8,128)} broadcast(f32[]{:T(128)} %constant.191.clone.1), dimensions={} | broadcast | bytes 6291460 | tf_op jit(solution)/shard_map/broadcast.11
  152.9 34.5 %while.45 = (s32[]{:T(128)}, f32[2,4,128,1536]{3,2,1,0:T(8,128)}, bf16[2,4,2,128,128]{4,3,2,1,0:T(8,128)(2,1)}, s32[2,4,2]{1,0,2:T(2,128)S(1)}, f32[16,12]{1,0:T(8,128)S(1)}, /*index=5*/f32[16,128,128]{1,2,0:T(8,128)}, s32[]{:T(128)}) while((s32[]{:T(128)}, f32[2,4,128,1536]{3,2,1,0:T(8,128)}, ...), condition=%wide.region_3.5_spmd.clone, body=%wide.region_2.4_spmd.clone.sunk | while | flops 410518592 | bytes 26482904 | solution.py:48
  153.2 4.9 %multiply_convert_fusion.9 = bf16[16,128,128,12]{1,2,3,0:T(8,128)(2,1)} fusion(f32[16,12]{1,0:T(8,128)S(1)} %get-tuple-element.509, f32[16,128,128]{1,2,0:T(8,128)} %get-tuple-element.510), kind=kLoop, calls=%fused_computation.22.clone.1 | loop fusion | flops 6291456 | bytes 7340800 | tf_op jit(solution)/shard_map/convert_element_type | solution.py:31
  158.1 5.4 %gather_fusion.1 = bf16[8,128,1536]{1,2,0:T(8,128)(2,1)} fusion(bf16[16,128,1536]{1,2,0:T(8,128)(2,1)} %bitcast.163, s32[1024]{0:T(1024)S(1)} %pad_clamp_fusion.9), kind=kCustom, calls=%fused_computation.1.clone.clone.1 | custom fusion | bytes 6291488 | tf_op jit(solution)/shard_map/while/body/eval_jaxpr/jit(_take)/gather | solution.py:45
  166.8 3.3 %fusion.83 = f32[2,4,128,1536]{3,2,1,0:T(8,128)} fusion(f32[2,4,128,1536]{3,2,1,0:T(8,128)} %get-tuple-element.499, s32[]{:T(128)S(6)} %copy.92, bf16[4,2,128,1536]{3,2,1,0:T(8,128)(2,1)S(1)} %copy.60, pred[4,2]{1,0:T(4,128)(4,1)S(1)} %copy.61, bf16[2,4,2,128,128]{4,3,2,1,0:T(8,128)(2,1)} %get-tuple-element.507), kind=kOutput, calls=%fused_computation.24.clone.1 | convolution fusion | flops 404226048 | bytes 6554632 | tf_op jit(solution)/shard_map/while/body/eval_jaxpr/rtab,rtbn->ran/dot_general | solution.py:46
  170.4 4.9 %multiply_convert_fusion.9 = bf16[16,128,128,12]{1,2,3,0:T(8,128)(2,1)} fusion(f32[16,12]{1,0:T(8,128)S(1)} %get-tuple-element.509, f32[16,128,128]{1,2,0:T(8,128)} %get-tuple-element.510), kind=kLoop, calls=%fused_computation.22.clone.1 | loop fusion | flops 6291456 | bytes 7340800 | tf_op jit(solution)/shard_map/convert_element_type | solution.py:31
  175.4 5.4 %gather_fusion.1 = bf16[8,128,1536]{1,2,0:T(8,128)(2,1)} fusion(bf16[16,128,1536]{1,2,0:T(8,128)(2,1)} %bitcast.163, s32[1024]{0:T(1024)S(1)} %pad_clamp_fusion.9), kind=kCustom, calls=%fused_computation.1.clone.clone.1 | custom fusion | bytes 6291488 | tf_op jit(solution)/shard_map/while/body/eval_jaxpr/jit(_take)/gather | solution.py:45
  184.0 3.4 %fusion.83 = f32[2,4,128,1536]{3,2,1,0:T(8,128)} fusion(f32[2,4,128,1536]{3,2,1,0:T(8,128)} %get-tuple-element.499, s32[]{:T(128)S(6)} %copy.92, bf16[4,2,128,1536]{3,2,1,0:T(8,128)(2,1)S(1)} %copy.60, pred[4,2]{1,0:T(4,128)(4,1)S(1)} %copy.61, bf16[2,4,2,128,128]{4,3,2,1,0:T(8,128)(2,1)} %get-tuple-element.507), kind=kOutput, calls=%fused_computation.24.clone.1 | convolution fusion | flops 404226048 | bytes 6554632 | tf_op jit(solution)/shard_map/while/body/eval_jaxpr/rtab,rtbn->ran/dot_general | solution.py:46
  187.7 3.7 %fusion.40 = bf16[4,16,1,128,128]{3,4,1,2,0:T(8,128)(2,1)} fusion(s32[]{:T(128)S(6)} %select_n.231, bf16[4,16,1,128,128]{3,4,1,2,0:T(8,128)(2,1)} %collective-permute-done.15), kind=kLoop, calls=%fused_computation.78 | loop fusion | flops 1048576 | bytes 4194308 | tf_op jit(solution)/shard_map/concatenate | solution.py:63
  195.2 3.4 %broadcast.166.clone.1 = f32[2,4,128,1536]{3,2,1,0:T(8,128)} broadcast(f32[]{:T(128)} %constant.191.clone.1), dimensions={} | broadcast | bytes 6291460 | tf_op jit(solution)/shard_map/broadcast.11
  198.6 34.5 %while.46 = (s32[]{:T(128)}, f32[2,4,128,1536]{3,2,1,0:T(8,128)}, bf16[2,4,2,128,128]{4,3,2,1,0:T(8,128)(2,1)}, s32[2,4,2]{1,0,2:T(2,128)S(1)}, f32[16,12]{1,0:T(8,128)S(1)}, /*index=5*/f32[16,128,128]{1,2,0:T(8,128)}, s32[]{:T(128)}) while((s32[]{:T(128)}, f32[2,4,128,1536]{3,2,1,0:T(8,128)}, ...), condition=%wide.region_5.7_spmd.clone, body=%wide.region_4.6_spmd.clone.sunk | while | flops 410518592 | bytes 26482904 | solution.py:48
  198.9 5.0 %multiply_convert_fusion.10 = bf16[16,128,128,12]{1,2,3,0:T(8,128)(2,1)} fusion(f32[16,12]{1,0:T(8,128)S(1)} %get-tuple-element.467, f32[16,128,128]{1,2,0:T(8,128)} %get-tuple-element.468), kind=kLoop, calls=%fused_computation.36.clone.1 | loop fusion | flops 6291456 | bytes 7340800 | tf_op jit(solution)/shard_map/convert_element_type | solution.py:31
  203.8 5.4 %gather_fusion.2 = bf16[8,128,1536]{1,2,0:T(8,128)(2,1)} fusion(bf16[16,128,1536]{1,2,0:T(8,128)(2,1)} %bitcast.164, s32[1024]{0:T(1024)S(1)} %pad_clamp_fusion.10), kind=kCustom, calls=%fused_computation.2.clone.clone.1 | custom fusion | bytes 6291488 | tf_op jit(solution)/shard_map/while/body/eval_jaxpr/jit(_take)/gather | solution.py:45
  212.5 3.3 %fusion.86 = f32[2,4,128,1536]{3,2,1,0:T(8,128)} fusion(f32[2,4,128,1536]{3,2,1,0:T(8,128)} %get-tuple-element.457, s32[]{:T(128)S(6)} %copy.80, bf16[4,2,128,1536]{3,2,1,0:T(8,128)(2,1)S(1)} %copy.63, pred[4,2]{1,0:T(4,128)(4,1)S(1)} %copy.64, bf16[2,4,2,128,128]{4,3,2,1,0:T(8,128)(2,1)} %get-tuple-element.465), kind=kOutput, calls=%fused_computation.38.clone.1 | convolution fusion | flops 404226048 | bytes 6554632 | tf_op jit(solution)/shard_map/while/body/eval_jaxpr/rtab,rtbn->ran/dot_general | solution.py:46
  216.1 5.0 %multiply_convert_fusion.10 = bf16[16,128,128,12]{1,2,3,0:T(8,128)(2,1)} fusion(f32[16,12]{1,0:T(8,128)S(1)} %get-tuple-element.467, f32[16,128,128]{1,2,0:T(8,128)} %get-tuple-element.468), kind=kLoop, calls=%fused_computation.36.clone.1 | loop fusion | flops 6291456 | bytes 7340800 | tf_op jit(solution)/shard_map/convert_element_type | solution.py:31
  221.1 5.4 %gather_fusion.2 = bf16[8,128,1536]{1,2,0:T(8,128)(2,1)} fusion(bf16[16,128,1536]{1,2,0:T(8,128)(2,1)} %bitcast.164, s32[1024]{0:T(1024)S(1)} %pad_clamp_fusion.10), kind=kCustom, calls=%fused_computation.2.clone.clone.1 | custom fusion | bytes 6291488 | tf_op jit(solution)/shard_map/while/body/eval_jaxpr/jit(_take)/gather | solution.py:45
  229.7 3.3 %fusion.86 = f32[2,4,128,1536]{3,2,1,0:T(8,128)} fusion(f32[2,4,128,1536]{3,2,1,0:T(8,128)} %get-tuple-element.457, s32[]{:T(128)S(6)} %copy.80, bf16[4,2,128,1536]{3,2,1,0:T(8,128)(2,1)S(1)} %copy.63, pred[4,2]{1,0:T(4,128)(4,1)S(1)} %copy.64, bf16[2,4,2,128,128]{4,3,2,1,0:T(8,128)(2,1)} %get-tuple-element.465), kind=kOutput, calls=%fused_computation.38.clone.1 | convolution fusion | flops 404226048 | bytes 6554632 | tf_op jit(solution)/shard_map/while/body/eval_jaxpr/rtab,rtbn->ran/dot_general | solution.py:46
  235.3 3.4 %broadcast.166.clone = f32[2,4,128,1536]{3,2,1,0:T(8,128)} broadcast(f32[]{:T(128)} %constant.191.clone.1), dimensions={} | broadcast | bytes 6291460 | tf_op jit(solution)/shard_map/broadcast.11
  238.7 34.3 %while.47 = (s32[]{:T(128)}, f32[2,4,128,1536]{3,2,1,0:T(8,128)}, bf16[2,4,2,128,128]{4,3,2,1,0:T(8,128)(2,1)}, s32[2,4,2]{1,0,2:T(2,128)S(1)}, f32[16,12]{1,0:T(8,128)S(1)}, /*index=5*/f32[16,128,128]{1,2,0:T(8,128)}, s32[]{:T(128)}) while((s32[]{:T(128)}, f32[2,4,128,1536]{3,2,1,0:T(8,128)}, ...), condition=%wide.region_7.9_spmd.clone, body=%wide.region_6.8_spmd.clone.sunk | while | flops 410518592 | bytes 26482904 | solution.py:48
  239.0 4.9 %multiply_convert_fusion.11 = bf16[16,128,128,12]{1,2,3,0:T(8,128)(2,1)} fusion(f32[16,12]{1,0:T(8,128)S(1)} %get-tuple-element.446, f32[16,128,128]{1,2,0:T(8,128)} %get-tuple-element.447), kind=kLoop, calls=%fused_computation.50.clone.1 | loop fusion | flops 6291456 | bytes 7340800 | tf_op jit(solution)/shard_map/convert_element_type | solution.py:31
  243.9 5.4 %gather_fusion.3 = bf16[8,128,1536]{1,2,0:T(8,128)(2,1)} fusion(bf16[16,128,1536]{1,2,0:T(8,128)(2,1)} %bitcast.165, s32[1024]{0:T(1024)S(1)} %pad_clamp_fusion.11), kind=kCustom, calls=%fused_computation.3.clone.clone.1 | custom fusion | bytes 6291488 | tf_op jit(solution)/shard_map/while/body/eval_jaxpr/jit(_take)/gather | solution.py:45
  252.5 3.4 %fusion.89 = f32[2,4,128,1536]{3,2,1,0:T(8,128)} fusion(f32[2,4,128,1536]{3,2,1,0:T(8,128)} %get-tuple-element.436, s32[]{:T(128)S(6)} %copy.74, bf16[4,2,128,1536]{3,2,1,0:T(8,128)(2,1)S(1)} %copy.66, pred[4,2]{1,0:T(4,128)(4,1)S(1)} %copy.67, bf16[2,4,2,128,128]{4,3,2,1,0:T(8,128)(2,1)} %get-tuple-element.444), kind=kOutput, calls=%fused_computation.52.clone.1 | convolution fusion | flops 404226048 | bytes 6554632 | tf_op jit(solution)/shard_map/while/body/eval_jaxpr/rtab,rtbn->ran/dot_general | solution.py:46
  256.2 4.9 %multiply_convert_fusion.11 = bf16[16,128,128,12]{1,2,3,0:T(8,128)(2,1)} fusion(f32[16,12]{1,0:T(8,128)S(1)} %get-tuple-element.446, f32[16,128,128]{1,2,0:T(8,128)} %get-tuple-element.447), kind=kLoop, calls=%fused_computation.50.clone.1 | loop fusion | flops 6291456 | bytes 7340800 | tf_op jit(solution)/shard_map/convert_element_type | solution.py:31
  261.1 5.4 %gather_fusion.3 = bf16[8,128,1536]{1,2,0:T(8,128)(2,1)} fusion(bf16[16,128,1536]{1,2,0:T(8,128)(2,1)} %bitcast.165, s32[1024]{0:T(1024)S(1)} %pad_clamp_fusion.11), kind=kCustom, calls=%fused_computation.3.clone.clone.1 | custom fusion | bytes 6291488 | tf_op jit(solution)/shard_map/while/body/eval_jaxpr/jit(_take)/gather | solution.py:45
  269.6 3.4 %fusion.89 = f32[2,4,128,1536]{3,2,1,0:T(8,128)} fusion(f32[2,4,128,1536]{3,2,1,0:T(8,128)} %get-tuple-element.436, s32[]{:T(128)S(6)} %copy.74, bf16[4,2,128,1536]{3,2,1,0:T(8,128)(2,1)S(1)} %copy.66, pred[4,2]{1,0:T(4,128)(4,1)S(1)} %copy.67, bf16[2,4,2,128,128]{4,3,2,1,0:T(8,128)(2,1)} %get-tuple-element.444), kind=kOutput, calls=%fused_computation.52.clone.1 | convolution fusion | flops 404226048 | bytes 6554632 | tf_op jit(solution)/shard_map/while/body/eval_jaxpr/rtab,rtbn->ran/dot_general | solution.py:46
  273.0 13.8 %add_add_fusion = f32[2,4,128,1536]{3,2,1,0:T(8,128)} fusion(f32[2,4,128,1536]{3,2,1,0:T(8,128)} %get-tuple-element.117, f32[2,4,128,1536]{3,2,1,0:T(8,128)} %get-tuple-element.116, f32[2,4,128,1536]{3,2,1,0:T(8,128)} %get-tuple-element.114, f32[2,4,128,1536]{3,2,1,0:T(8,128)} %get-tuple-element.115), kind=kLoop, calls=%fused_computation.64 | loop fusion | flops 4718592 | bytes 31457280 | tf_op jit(solution)/shard_map/add | solution.py:117
  286.8 20.3 %all-reduce.1 = bf16[1024,1536]{1,0:T(8,128)(2,1)S(1)} all-reduce(f32[1024,1536]{1,0:T(8,128)} %bitcast.170), channel_id=1, replica_groups=mesh['row'=2,'col'=8,'depth'=2] {'depth'}, use_global_device_ids=true, to_apply=%region_8.10 | all-reduce | flops 1572864 | bytes 9437184 | tf_op jit(solution)/shard_map/psum | solution.py:131
  (169 shorter events, 70.9 us)
Async XLA Ops:
  0.0 14.7 %copy-start.4 = (s32[1,1,8]{2,1,0:T(1,128)S(1)}, s32[1,1,8]{2,1,0:T(1,128)}, u32[]{:S(2)}) copy-start(s32[1,1,8]{2,1,0:T(1,128)} %param.18) | copy-start | bytes 100
  0.0 15.3 %copy-start.3 = (s32[1,1,8,2]{2,3,1,0:T(2,128)S(1)}, s32[1,1,8,2]{2,3,1,0:T(2,128)}, u32[]{:S(2)}) copy-start(s32[1,1,8,2]{2,3,1,0:T(2,128)} %param.17) | copy-start | bytes 196
  0.0 50.9 %copy-start.1 = (s32[4,1,1,1,16,1]{4,5,3,2,1,0:T(1,128)S(1)}, s32[4,1,1,1,16,1]{4,5,3,2,1,0:T(1,128)}, u32[]{:S(2)}) copy-start(s32[4,1,1,1,16,1]{4,5,3,2,1,0:T(1,128)} %param.20) | copy-start | bytes 772
  0.0 52.6 %copy-start.2 = (s32[4,1,1,1,16]{4,3,2,1,0:T(1,128)S(1)}, s32[4,1,1,1,16]{4,3,2,1,0:T(1,128)}, u32[]{:S(2)}) copy-start(s32[4,1,1,1,16]{4,3,2,1,0:T(1,128)} %param.21) | copy-start | bytes 772
  0.0 66.7 %copy-start = (bf16[1,1,8,2,128,128]{5,4,3,2,1,0:T(8,128)(2,1)S(1)}, bf16[1,1,8,2,128,128]{5,4,3,2,1,0:T(8,128)(2,1)}, u32[]{:S(2)}) copy-start(bf16[1,1,8,2,128,128]{5,4,3,2,1,0:T(8,128)(2,1)} %param.16) | copy-start | bytes 1572868
  0.0 13.1 %collective-permute-start = (s32[8]{0:T(128)}, s32[8]{0:T(128)S(1)}, u32[]{:S(2)}, u32[]{:S(2)}) collective-permute-start(s32[8]{0:T(128)} %bitcast.190), channel_id=1, source_target_pairs={{0,14},{2,0},{4,2},{6,4},{8,6},{10,8},{12,10},{14,12},{1,15},{3,1}... | collective-permute-start | bytes 104 | tf_op jit(solution)/shard_map/ppermute | solution.py:18
  6.1 8.7 %collective-permute-start.2 = (s32[8,2]{0,1:T(2,128)}, s32[8,2]{0,1:T(2,128)S(1)}, u32[]{:S(2)}, u32[]{:S(2)}) collective-permute-start(s32[8,2]{0,1:T(2,128)} %bitcast.189), channel_id=1, source_target_pairs={{0,14},{2,0},{4,2},{6,4},{8,6},{10,8},{12,10},{14,12},{1,15},{3,1}... | collective-permute-start | bytes 200 | tf_op jit(solution)/shard_map/ppermute | solution.py:18
  6.6 44.3 %collective-permute-start.4 = (s32[4,16,1]{1,0,2:T(4,128)}, s32[4,16,1]{1,0,2:T(4,128)S(1)}, u32[]{:S(2)}, u32[]{:S(2)}) collective-permute-start(s32[4,16,1]{1,0,2:T(4,128)} %bitcast.185), channel_id=1, source_target_pairs={{0,16},{16,0},{1,17},{17,1},{2,18},{18,2},{3,19},{19,3},{4,20},{20... | collective-permute-start | bytes 776 | tf_op jit(solution)/shard_map/ppermute | solution.py:18
  8.1 44.4 %collective-permute-start.5 = (s32[4,16]{1,0:T(4,128)}, s32[4,16]{1,0:T(4,128)S(1)}, u32[]{:S(2)}, u32[]{:S(2)}) collective-permute-start(s32[4,16]{1,0:T(4,128)} %bitcast.187), channel_id=1, source_target_pairs={{0,16},{16,0},{1,17},{17,1},{2,18},{18,2},{3,19},{19,3},{4,20},{20... | collective-permute-start | bytes 776 | tf_op jit(solution)/shard_map/ppermute | solution.py:18
  8.6 58.0 %collective-permute-start.1 = (bf16[8,2,128,128]{3,2,1,0:T(8,128)(2,1)}, bf16[8,2,128,128]{3,2,1,0:T(8,128)(2,1)S(1)}, u32[]{:S(2)}, u32[]{:S(2)}) collective-permute-start(bf16[8,2,128,128]{3,2,1,0:T(8,128)(2,1)} %bitcast.176), channel_id=1, source_target_pairs={{0,14},{2,0},{4,2},{6,4},{8,6},{10,8},{12,10},{14,12},{1,15},{3,1}... | collective-permute-start | bytes 1572872 | tf_op jit(solution)/shard_map/ppermute | solution.py:18
  13.1 82.0 %collective-permute-start.3 = (bf16[4,16,1,128,128]{3,4,1,2,0:T(8,128)(2,1)S(1)}, bf16[4,16,1,128,128]{3,4,1,2,0:T(8,128)(2,1)}, u32[]{:S(2)}, u32[]{:S(2)}) collective-permute-start(bf16[4,16,1,128,128]{3,4,1,2,0:T(8,128)(2,1)S(1)} %bitcast.171), channel_id=1, source_target_pairs={{0,16},{16,0},{1,17},{17,1},{2,18},{18,2},{3,19},{19,3},{4,20},{20... | collective-permute-start | bytes 6291464 | tf_op jit(solution)/shard_map/ppermute | solution.py:18
  14.8 6.7 %collective-permute-start.6 = (s32[8]{0:T(128)S(1)}, s32[8]{0:T(128)S(1)}, u32[]{:S(2)}, u32[]{:S(2)}) collective-permute-start(s32[8]{0:T(128)S(1)} %broadcast_select_fusion.6), channel_id=1, source_target_pairs={{0,14},{2,0},{4,2},{6,4},{8,6},{10,8},{12,10},{14,12},{1,15},{3,1}... | collective-permute-start | bytes 104 | tf_op jit(solution)/shard_map/ppermute | solution.py:18
  21.6 5.4 %collective-permute-start.12 = (s32[8]{0:T(128)S(1)}, s32[8]{0:T(128)S(1)}, u32[]{:S(2)}, u32[]{:S(2)}) collective-permute-start(s32[8]{0:T(128)S(1)} %collective-permute-done.6), channel_id=1, source_target_pairs={{0,14},{2,0},{4,2},{6,4},{8,6},{10,8},{12,10},{14,12},{1,15},{3,1}... | collective-permute-start | bytes 104 | tf_op jit(solution)/shard_map/ppermute | solution.py:18
  27.0 6.3 %collective-permute-start.18 = (s32[8]{0:T(128)S(1)}, s32[8]{0:T(128)S(1)}, u32[]{:S(2)}, u32[]{:S(2)}) collective-permute-start(s32[8]{0:T(128)S(1)} %collective-permute-done.12), channel_id=1, source_target_pairs={{0,14},{2,0},{4,2},{6,4},{8,6},{10,8},{12,10},{14,12},{1,15},{3,1}... | collective-permute-start | bytes 104 | tf_op jit(solution)/shard_map/ppermute | solution.py:18
  33.3 6.3 %collective-permute-start.8 = (s32[8,2]{0,1:T(2,128)S(1)}, s32[8,2]{0,1:T(2,128)S(1)}, u32[]{:S(2)}, u32[]{:S(2)}) collective-permute-start(s32[8,2]{0,1:T(2,128)S(1)} %broadcast_select_fusion.5), channel_id=1, source_target_pairs={{0,14},{2,0},{4,2},{6,4},{8,6},{10,8},{12,10},{14,12},{1,15},{3,1}... | collective-permute-start | bytes 200 | tf_op jit(solution)/shard_map/ppermute | solution.py:18
  39.6 6.3 %collective-permute-start.14 = (s32[8,2]{0,1:T(2,128)S(1)}, s32[8,2]{0,1:T(2,128)S(1)}, u32[]{:S(2)}, u32[]{:S(2)}) collective-permute-start(s32[8,2]{0,1:T(2,128)S(1)} %collective-permute-done.8), channel_id=1, source_target_pairs={{0,14},{2,0},{4,2},{6,4},{8,6},{10,8},{12,10},{14,12},{1,15},{3,1}... | collective-permute-start | bytes 200 | tf_op jit(solution)/shard_map/ppermute | solution.py:18
  45.9 7.4 %collective-permute-start.20 = (s32[8,2]{0,1:T(2,128)S(1)}, s32[8,2]{0,1:T(2,128)S(1)}, u32[]{:S(2)}, u32[]{:S(2)}) collective-permute-start(s32[8,2]{0,1:T(2,128)S(1)} %collective-permute-done.14), channel_id=1, source_target_pairs={{0,14},{2,0},{4,2},{6,4},{8,6},{10,8},{12,10},{14,12},{1,15},{3,1}... | collective-permute-start | bytes 200 | tf_op jit(solution)/shard_map/ppermute | solution.py:18
  51.0 8.3 %collective-permute-start.10 = (s32[4,16,1]{1,0,2:T(4,128)S(1)}, s32[4,16,1]{1,0,2:T(4,128)S(1)}, u32[]{:S(2)}, u32[]{:S(2)}) collective-permute-start(s32[4,16,1]{1,0,2:T(4,128)S(1)} %fusion.62), channel_id=1, source_target_pairs={{0,16},{16,0},{1,17},{17,1},{2,18},{18,2},{3,19},{19,3},{4,20},{20... | collective-permute-start | bytes 776 | tf_op jit(solution)/shard_map/ppermute | solution.py:18
  52.7 8.2 %collective-permute-start.11 = (s32[4,16]{1,0:T(4,128)S(1)}, s32[4,16]{1,0:T(4,128)S(1)}, u32[]{:S(2)}, u32[]{:S(2)}) collective-permute-start(s32[4,16]{1,0:T(4,128)S(1)} %fusion.65), channel_id=1, source_target_pairs={{0,16},{16,0},{1,17},{17,1},{2,18},{18,2},{3,19},{19,3},{4,20},{20... | collective-permute-start | bytes 776 | tf_op jit(solution)/shard_map/ppermute | solution.py:18
  59.3 3.7 %collective-permute-start.16 = (s32[4,16,1]{1,0,2:T(4,128)S(1)}, s32[4,16,1]{1,0,2:T(4,128)S(1)}, u32[]{:S(2)}, u32[]{:S(2)}) collective-permute-start(s32[4,16,1]{1,0,2:T(4,128)S(1)} %constant_dynamic-slice_fusion.9), channel_id=1, source_target_pairs={{0,16},{16,0},{1,17},{17,1},{2,18},{18,2},{3,19},{19,3},{4,20},{20... | collective-permute-start | bytes 776 | tf_op jit(solution)/shard_map/ppermute | solution.py:18
  60.9 3.7 %collective-permute-start.17 = (s32[4,16]{1,0:T(4,128)S(1)}, s32[4,16]{1,0:T(4,128)S(1)}, u32[]{:S(2)}, u32[]{:S(2)}) collective-permute-start(s32[4,16]{1,0:T(4,128)S(1)} %constant_dynamic-slice_fusion.8), channel_id=1, source_target_pairs={{0,16},{16,0},{1,17},{17,1},{2,18},{18,2},{3,19},{19,3},{4,20},{20... | collective-permute-start | bytes 776 | tf_op jit(solution)/shard_map/ppermute | solution.py:18
  63.0 3.7 %collective-permute-start.22 = (s32[4,16,1]{1,0,2:T(4,128)S(1)}, s32[4,16,1]{1,0,2:T(4,128)S(1)}, u32[]{:S(2)}, u32[]{:S(2)}) collective-permute-start(s32[4,16,1]{1,0,2:T(4,128)S(1)} %constant_dynamic-slice_fusion.7), channel_id=1, source_target_pairs={{0,16},{16,0},{1,17},{17,1},{2,18},{18,2},{3,19},{19,3},{4,20},{20... | collective-permute-start | bytes 776 | tf_op jit(solution)/shard_map/ppermute | solution.py:18
  64.6 3.7 %collective-permute-start.23 = (s32[4,16]{1,0:T(4,128)S(1)}, s32[4,16]{1,0:T(4,128)S(1)}, u32[]{:S(2)}, u32[]{:S(2)}) collective-permute-start(s32[4,16]{1,0:T(4,128)S(1)} %constant_dynamic-slice_fusion.6), channel_id=1, source_target_pairs={{0,16},{16,0},{1,17},{17,1},{2,18},{18,2},{3,19},{19,3},{4,20},{20... | collective-permute-start | bytes 776 | tf_op jit(solution)/shard_map/ppermute | solution.py:18
  67.6 12.5 %collective-permute-start.7 = (bf16[8,2,128,128]{3,2,1,0:T(8,128)(2,1)S(1)}, bf16[8,2,128,128]{3,2,1,0:T(8,128)(2,1)S(1)}, u32[]{:S(2)}, u32[]{:S(2)}) collective-permute-start(bf16[8,2,128,128]{3,2,1,0:T(8,128)(2,1)S(1)} %get-tuple-element.279), channel_id=1, source_target_pairs={{0,14},{2,0},{4,2},{6,4},{8,6},{10,8},{12,10},{14,12},{1,15},{3,1}... | collective-permute-start | bytes 1572872 | tf_op jit(solution)/shard_map/ppermute | solution.py:18
  80.0 13.6 %collective-permute-start.13 = (bf16[8,2,128,128]{3,2,1,0:T(8,128)(2,1)S(1)}, bf16[8,2,128,128]{3,2,1,0:T(8,128)(2,1)S(1)}, u32[]{:S(2)}, u32[]{:S(2)}) collective-permute-start(bf16[8,2,128,128]{3,2,1,0:T(8,128)(2,1)S(1)} %collective-permute-done.7), channel_id=1, source_target_pairs={{0,14},{2,0},{4,2},{6,4},{8,6},{10,8},{12,10},{14,12},{1,15},{3,1}... | collective-permute-start | bytes 1572872 | tf_op jit(solution)/shard_map/ppermute | solution.py:18
  93.6 10.5 %collective-permute-start.19 = (bf16[8,2,128,128]{3,2,1,0:T(8,128)(2,1)S(1)}, bf16[8,2,128,128]{3,2,1,0:T(8,128)(2,1)S(1)}, u32[]{:S(2)}, u32[]{:S(2)}) collective-permute-start(bf16[8,2,128,128]{3,2,1,0:T(8,128)(2,1)S(1)} %collective-permute-done.13), channel_id=1, source_target_pairs={{0,14},{2,0},{4,2},{6,4},{8,6},{10,8},{12,10},{14,12},{1,15},{3,1}... | collective-permute-start | bytes 1572872 | tf_op jit(solution)/shard_map/ppermute | solution.py:18
  100.6 42.5 %collective-permute-start.9 = (bf16[4,16,1,128,128]{3,4,1,2,0:T(8,128)(2,1)}, bf16[4,16,1,128,128]{3,4,1,2,0:T(8,128)(2,1)}, u32[]{:S(2)}, u32[]{:S(2)}) collective-permute-start(bf16[4,16,1,128,128]{3,4,1,2,0:T(8,128)(2,1)} %fusion.43), channel_id=1, source_target_pairs={{0,16},{16,0},{1,17},{17,1},{2,18},{18,2},{3,19},{19,3},{4,20},{20... | collective-permute-start | bytes 6291464 | tf_op jit(solution)/shard_map/ppermute | solution.py:18
  148.9 38.8 %collective-permute-start.15 = (bf16[4,16,1,128,128]{3,4,1,2,0:T(8,128)(2,1)}, bf16[4,16,1,128,128]{3,4,1,2,0:T(8,128)(2,1)}, u32[]{:S(2)}, u32[]{:S(2)}) collective-permute-start(bf16[4,16,1,128,128]{3,4,1,2,0:T(8,128)(2,1)} %fusion.41), channel_id=1, source_target_pairs={{0,16},{16,0},{1,17},{17,1},{2,18},{18,2},{3,19},{19,3},{4,20},{20... | collective-permute-start | bytes 6291464 | tf_op jit(solution)/shard_map/ppermute | solution.py:18
  193.5 39.5 %collective-permute-start.21 = (bf16[4,16,1,128,128]{3,4,1,2,0:T(8,128)(2,1)}, bf16[4,16,1,128,128]{3,4,1,2,0:T(8,128)(2,1)}, u32[]{:S(2)}, u32[]{:S(2)}) collective-permute-start(bf16[4,16,1,128,128]{3,4,1,2,0:T(8,128)(2,1)} %fusion.40), channel_id=1, source_target_pairs={{0,16},{16,0},{1,17},{17,1},{2,18},{18,2},{3,19},{19,3},{4,20},{20... | collective-permute-start | bytes 6291464 | tf_op jit(solution)/shard_map/ppermute | solution.py:18
where the time goes:
time: 310 us; the launch traced here: 308 us
  local copies, waits for them, and re-layouts  89.5 us (29%)
  other arithmetic  79.5 us (26%)
  starting transfers between devices  47.8 us (15%)
  waiting for transfers between devices  44.1 us (14%)
  matrix products  26.8 us (9%)
  blocking collectives  20.3 us (7%)
    gather x16, local copies, waits for them, and re-layouts, one_group(): chosen = jnp.take(rows_dense, cols_part, axis=0)  68.8 us
    ppermute x24, starting transfers between devices, shifted(): return lax.ppermute(value, axis, pairs)  47.8 us
    ppermute x24, waiting for transfers between devices, shifted(): return lax.ppermute(value, axis, pairs)  44.1 us
    convert_element_type x8, other arithmetic, dense_panel(): spread.astype(jnp.bfloat16)  39.5 us
    dot_general x8, matrix products, one_group(): jnp.einsum('rtab,rtbn->ran', tiles_part, chosen, preferred_element_type=j...  26.8 us
    psum x1, blocking collectives, local(): summed = lax.psum(flat_running, 'depth')  20.3 us
    add x1, other arithmetic, local(): running = running + panel_product(tiles_a, cols_a, count_a, rows_dense)  13.8 us
    another operation x4, local copies, waits for them, and re-layouts  13.7 us
  transfers between devices with their start and end apart: 24, of which 12 were waited for; matrix products, arithmetic and copies ran while one was open for 42% of the time, Pallas kernels for 0%

commit v1 on v0

--- a/solution.py
+++ b/solution.py
@@ -6,6 +6,11 @@
 
 BC = 12
 SHIFTS = 4
+
+
+def change_meshes_over_axis(state):
+    reply = lax.all_gather(state, "depth").sum(axis=0)
+    return reply
 
 
 def for_sending(array):
@@ -128,7 +133,7 @@
             )
             tiles_b, cols_b, count_b = roll_slots(moved, (row_group + 1) // rows_axis)
     flat_running = running.reshape(-1, running.shape[2])
-    summed = lax.psum(flat_running, "depth")
+    summed = change_meshes_over_axis(flat_running)
     half_rows = flat_running.shape[0] // lax.axis_size("depth")
     own_rows = lax.dynamic_slice_in_dim(summed, lax.axis_index("depth") * half_rows, half_rows, 0)
     return own_rows.astype(jnp.bfloat16)

time: 310 us -> 346 us (1.12)
  blocking collectives: 20.3 us -> 0 us
  starting transfers between devices: 47.8 us -> 66.1 us
  waiting for transfers between devices: 44.1 us -> 62.1 us
  between operations: 0.27 us -> 13.6 us
  other arithmetic: 79.5 us -> 85.9 us
    all_gather x0 -> x1, waiting for transfers between devices: none -> 23.5 us  [change_meshes_over_axis(): reply = lax.all_gather(state, 'depth').sum(axis=0)]
    psum x1 -> x0, blocking collectives: 20.3 us -> none  [local(): summed = lax.psum(flat_running, 'depth')]
    ppermute x24, starting transfers between devices: 47.8 us -> 66 us  [shifted(): return lax.ppermute(value, axis, pairs)]
    reduce_sum x0 -> x1, other arithmetic: none -> 6.57 us  [change_meshes_over_axis(): reply = lax.all_gather(state, 'depth').sum(axis=0)]
    ppermute x24, waiting for transfers between devices: 44.1 us -> 38.7 us  [shifted(): return lax.ppermute(value, axis, pairs)]
  transfers between devices with their start and end apart: 24 -> 25, of which waited for: 12 -> 15; matrix products, arithmetic and copies ran while one was open for 42% -> 37% of each run, Pallas kernels for 0% -> 0%
where the time goes in v1:
time: 346 us; the launch traced here: 344 us
  local copies, waits for them, and re-layouts  89.6 us (26%)
  other arithmetic  85.9 us (25%)
  starting transfers between devices  66.1 us (19%)
  waiting for transfers between devices  62.1 us (18%)
  matrix products  26.8 us (8%)
  between operations  13.6 us (4%)
    gather x16, local copies, waits for them, and re-layouts, one_group(): chosen = jnp.take(rows_dense, cols_part, axis=0)  68.7 us
    ppermute x24, starting transfers between devices, shifted(): return lax.ppermute(value, axis, pairs)  66 us
    convert_element_type x8, other arithmetic, dense_panel(): spread.astype(jnp.bfloat16)  39.5 us
    ppermute x24, waiting for transfers between devices, shifted(): return lax.ppermute(value, axis, pairs)  38.7 us
    dot_general x8, matrix products, one_group(): jnp.einsum('rtab,rtbn->ran', tiles_part, chosen, preferred_element_type=j...  26.8 us
    all_gather x1, waiting for transfers between devices, change_meshes_over_axis(): reply = lax.all_gather(state, 'depth').sum(axis=0)  23.5 us
    add x1, other arithmetic, local(): running = running + panel_product(tiles_a, cols_a, count_a, rows_dense)  13.8 us
    another operation x4, local copies, waits for them, and re-layouts  13.7 us
  transfers between devices with their start and end apart: 25, of which 15 were waited for; matrix products, arithmetic and copies ran while one was open for 37% of the time, Pallas kernels for 0%

profile of v1, /device:TPU:0, one launch (start us, length us, event | category | flops | bytes accessed | tf_op | source)
XLA Modules:
  0.0 344.3 jit_solution(11527402594995335450)
XLA Ops:
  14.8 4.5 %collective-permute-start = (s32[8]{0:T(128)S(1)}, s32[8]{0:T(128)S(1)}, u32[]{:S(2)}, u32[]{:S(2)}) collective-permute-start(s32[8]{0:T(128)S(1)} %bitcast.190), channel_id=1, source_target_pairs={{0,14},{2,0},{4,2},{6,4},{8,6},{10,8},{12,10},{14,12},{1,15},{3,1}... | collective-permute-start | bytes 104 | tf_op jit(solution)/shard_map/ppermute | solution.py:23
  20.7 5.0 %collective-permute-start.2 = (s32[8,2]{0,1:T(2,128)S(1)}, s32[8,2]{0,1:T(2,128)S(1)}, u32[]{:S(2)}, u32[]{:S(2)}) collective-permute-start(s32[8,2]{0,1:T(2,128)S(1)} %bitcast.189), channel_id=1, source_target_pairs={{0,14},{2,0},{4,2},{6,4},{8,6},{10,8},{12,10},{14,12},{1,15},{3,1}... | collective-permute-start | bytes 200 | tf_op jit(solution)/shard_map/ppermute | solution.py:23
  25.7 6.3 %collective-permute-done.2 = s32[8,2]{0,1:T(2,128)S(1)} collective-permute-done((s32[8,2]{0,1:T(2,128)S(1)}, s32[8,2]{0,1:T(2,128)S(1)}, u32[]{:S(2)}, u32[]{:S(2)}) %collective-permute-start.2) | collective-permute-done | bytes 96 | tf_op jit(solution)/shard_map/ppermute | solution.py:23
  36.6 5.0 %collective-permute-start.12 = (s32[8]{0:T(128)S(1)}, s32[8]{0:T(128)S(1)}, u32[]{:S(2)}, u32[]{:S(2)}) collective-permute-start(s32[8]{0:T(128)S(1)} %collective-permute-done.6), channel_id=1, source_target_pairs={{0,14},{2,0},{4,2},{6,4},{8,6},{10,8},{12,10},{14,12},{1,15},{3,1}... | collective-permute-start | bytes 104 | tf_op jit(solution)/shard_map/ppermute | solution.py:23
  42.8 5.0 %collective-permute-start.8 = (s32[8,2]{0,1:T(2,128)S(1)}, s32[8,2]{0,1:T(2,128)S(1)}, u32[]{:S(2)}, u32[]{:S(2)}) collective-permute-start(s32[8,2]{0,1:T(2,128)S(1)} %broadcast_select_fusion.5), channel_id=1, source_target_pairs={{0,14},{2,0},{4,2},{6,4},{8,6},{10,8},{12,10},{14,12},{1,15},{3,1}... | collective-permute-start | bytes 200 | tf_op jit(solution)/shard_map/ppermute | solution.py:23
  49.1 5.0 %collective-permute-start.18 = (s32[8]{0:T(128)S(1)}, s32[8]{0:T(128)S(1)}, u32[]{:S(2)}, u32[]{:S(2)}) collective-permute-start(s32[8]{0:T(128)S(1)} %collective-permute-done.12), channel_id=1, source_target_pairs={{0,14},{2,0},{4,2},{6,4},{8,6},{10,8},{12,10},{14,12},{1,15},{3,1}... | collective-permute-start | bytes 104 | tf_op jit(solution)/shard_map/ppermute | solution.py:23
  55.4 5.0 %collective-permute-start.14 = (s32[8,2]{0,1:T(2,128)S(1)}, s32[8,2]{0,1:T(2,128)S(1)}, u32[]{:S(2)}, u32[]{:S(2)}) collective-permute-start(s32[8,2]{0,1:T(2,128)S(1)} %collective-permute-done.8), channel_id=1, source_target_pairs={{0,14},{2,0},{4,2},{6,4},{8,6},{10,8},{12,10},{14,12},{1,15},{3,1}... | collective-permute-start | bytes 200 | tf_op jit(solution)/shard_map/ppermute | solution.py:23
  61.7 5.0 %collective-permute-start.20 = (s32[8,2]{0,1:T(2,128)S(1)}, s32[8,2]{0,1:T(2,128)S(1)}, u32[]{:S(2)}, u32[]{:S(2)}) collective-permute-start(s32[8,2]{0,1:T(2,128)S(1)} %collective-permute-done.14), channel_id=1, source_target_pairs={{0,14},{2,0},{4,2},{6,4},{8,6},{10,8},{12,10},{14,12},{1,15},{3,1}... | collective-permute-start | bytes 200 | tf_op jit(solution)/shard_map/ppermute | solution.py:23
  81.4 11.6 %collective-permute-done.7 = bf16[8,2,128,128]{3,2,1,0:T(8,128)(2,1)S(1)} collective-permute-done((bf16[8,2,128,128]{3,2,1,0:T(8,128)(2,1)S(1)}, bf16[8,2,128,128]{3,2,1,0:T(8,128)(2,1)S(1)}, u32[]{:S(2)}, u32[]{:S(2)}) %collective-permute-start.7) | collective-permute-done | bytes 524320 | tf_op jit(solution)/shard_map/ppermute | solution.py:23
  93.0 5.2 %collective-permute-start.13 = (bf16[8,2,128,128]{3,2,1,0:T(8,128)(2,1)S(1)}, bf16[8,2,128,128]{3,2,1,0:T(8,128)(2,1)S(1)}, u32[]{:S(2)}, u32[]{:S(2)}) collective-permute-start(bf16[8,2,128,128]{3,2,1,0:T(8,128)(2,1)S(1)} %collective-permute-done.7), channel_id=1, source_target_pairs={{0,14},{2,0},{4,2},{6,4},{8,6},{10,8},{12,10},{14,12},{1,15},{3,1}... | collective-permute-start | bytes 1572872 | tf_op jit(solution)/shard_map/ppermute | solution.py:23
  99.2 9.8 %collective-permute-done.13 = bf16[8,2,128,128]{3,2,1,0:T(8,128)(2,1)S(1)} collective-permute-done((bf16[8,2,128,128]{3,2,1,0:T(8,128)(2,1)S(1)}, bf16[8,2,128,128]{3,2,1,0:T(8,128)(2,1)S(1)}, u32[]{:S(2)}, u32[]{:S(2)}) %collective-permute-start.13) | collective-permute-done | bytes 524320 | tf_op jit(solution)/shard_map/ppermute | solution.py:23
  109.0 5.2 %collective-permute-start.19 = (bf16[8,2,128,128]{3,2,1,0:T(8,128)(2,1)S(1)}, bf16[8,2,128,128]{3,2,1,0:T(8,128)(2,1)S(1)}, u32[]{:S(2)}, u32[]{:S(2)}) collective-permute-start(bf16[8,2,128,128]{3,2,1,0:T(8,128)(2,1)S(1)} %collective-permute-done.13), channel_id=1, source_target_pairs={{0,14},{2,0},{4,2},{6,4},{8,6},{10,8},{12,10},{14,12},{1,15},{3,1}... | collective-permute-start | bytes 1572872 | tf_op jit(solution)/shard_map/ppermute | solution.py:23
  125.1 3.4 broadcast.166.clone.2
  128.5 34.6 %while.44 = (s32[]{:T(128)}, f32[2,4,128,1536]{3,2,1,0:T(8,128)}, bf16[2,4,2,128,128]{4,3,2,1,0:T(8,128)(2,1)}, s32[2,4,2]{1,0,2:T(2,128)S(1)}, f32[16,12]{1,0:T(8,128)S(1)}, /*index=5*/f32[16,128,128]{1,2,0:T(8,128)}, s32[]{:T(128)}) while((s32[]{:T(128)}, f32[2,4,128,1536]{3,2,1,0:T(8,128)}, ...), condition=%wide.region_1.3_spmd.clone, body=%wide.region_0.2_spmd.clone.sunk | while | flops 410518592 | bytes 26482896 | solution.py:53
  128.7 4.9 %multiply_convert_fusion.8 = bf16[16,128,128,12]{1,2,3,0:T(8,128)(2,1)} fusion(f32[16,12]{1,0:T(8,128)S(1)} %get-tuple-element.512, f32[16,128,128]{1,2,0:T(8,128)} %get-tuple-element.513), kind=kLoop, calls=%fused_computation.8.clone.1 | loop fusion | flops 6291456 | bytes 7340800 | tf_op jit(solution)/shard_map/convert_element_type | solution.py:36
  133.7 5.5 %gather_fusion = bf16[8,128,1536]{1,2,0:T(8,128)(2,1)} fusion(bf16[16,128,1536]{1,2,0:T(8,128)(2,1)} %bitcast.162, s32[1024]{0:T(1024)S(1)} %pad_clamp_fusion.8), kind=kCustom, calls=%fused_computation.clone.clone.1 | custom fusion | bytes 6291488 | tf_op jit(solution)/shard_map/while/body/eval_jaxpr/jit(_take)/gather | solution.py:50
  142.4 3.4 fusion.80
  146.0 4.9 %multiply_convert_fusion.8 = bf16[16,128,128,12]{1,2,3,0:T(8,128)(2,1)} fusion(f32[16,12]{1,0:T(8,128)S(1)} %get-tuple-element.512, f32[16,128,128]{1,2,0:T(8,128)} %get-tuple-element.513), kind=kLoop, calls=%fused_computation.8.clone.1 | loop fusion | flops 6291456 | bytes 7340800 | tf_op jit(solution)/shard_map/convert_element_type | solution.py:36
  151.0 5.5 %gather_fusion = bf16[8,128,1536]{1,2,0:T(8,128)(2,1)} fusion(bf16[16,128,1536]{1,2,0:T(8,128)(2,1)} %bitcast.162, s32[1024]{0:T(1024)S(1)} %pad_clamp_fusion.8), kind=kCustom, calls=%fused_computation.clone.clone.1 | custom fusion | bytes 6291488 | tf_op jit(solution)/shard_map/while/body/eval_jaxpr/jit(_take)/gather | solution.py:50
  159.7 3.4 fusion.80
  163.1 3.7 %fusion.41 = bf16[4,16,1,128,128]{3,4,1,2,0:T(8,128)(2,1)} fusion(s32[]{:T(128)S(6)} %select_n.231, bf16[4,16,1,128,128]{3,4,1,2,0:T(8,128)(2,1)} %collective-permute-done.9), kind=kLoop, calls=%fused_computation.79 | loop fusion | flops 1048576 | bytes 4194308 | tf_op jit(solution)/shard_map/concatenate | solution.py:68
  169.5 3.5 %broadcast.166.clone.3 = f32[2,4,128,1536]{3,2,1,0:T(8,128)} broadcast(f32[]{:T(128)} %constant.192.clone.1), dimensions={} | broadcast | bytes 6291460 | tf_op jit(solution)/shard_map/broadcast.11
  173.0 34.5 %while.45 = (s32[]{:T(128)}, f32[2,4,128,1536]{3,2,1,0:T(8,128)}, bf16[2,4,2,128,128]{4,3,2,1,0:T(8,128)(2,1)}, s32[2,4,2]{1,0,2:T(2,128)S(1)}, f32[16,12]{1,0:T(8,128)S(1)}, /*index=5*/f32[16,128,128]{1,2,0:T(8,128)}, s32[]{:T(128)}) while((s32[]{:T(128)}, f32[2,4,128,1536]{3,2,1,0:T(8,128)}, ...), condition=%wide.region_3.5_spmd.clone, body=%wide.region_2.4_spmd.clone.sunk | while | flops 410518592 | bytes 26482896 | solution.py:53
  173.2 4.9 %multiply_convert_fusion.9 = bf16[16,128,128,12]{1,2,3,0:T(8,128)(2,1)} fusion(f32[16,12]{1,0:T(8,128)S(1)} %get-tuple-element.533, f32[16,128,128]{1,2,0:T(8,128)} %get-tuple-element.534), kind=kLoop, calls=%fused_computation.22.clone.1 | loop fusion | flops 6291456 | bytes 7340800 | tf_op jit(solution)/shard_map/convert_element_type | solution.py:36
  178.1 5.5 %gather_fusion.1 = bf16[8,128,1536]{1,2,0:T(8,128)(2,1)} fusion(bf16[16,128,1536]{1,2,0:T(8,128)(2,1)} %bitcast.163, s32[1024]{0:T(1024)S(1)} %pad_clamp_fusion.9), kind=kCustom, calls=%fused_computation.1.clone.clone.1 | custom fusion | bytes 6291488 | tf_op jit(solution)/shard_map/while/body/eval_jaxpr/jit(_take)/gather | solution.py:50
  186.9 3.3 fusion.83
  190.4 4.9 %multiply_convert_fusion.9 = bf16[16,128,128,12]{1,2,3,0:T(8,128)(2,1)} fusion(f32[16,12]{1,0:T(8,128)S(1)} %get-tuple-element.533, f32[16,128,128]{1,2,0:T(8,128)} %get-tuple-element.534), kind=kLoop, calls=%fused_computation.22.clone.1 | loop fusion | flops 6291456 | bytes 7340800 | tf_op jit(solution)/shard_map/convert_element_type | solution.py:36
  195.3 5.5 %gather_fusion.1 = bf16[8,128,1536]{1,2,0:T(8,128)(2,1)} fusion(bf16[16,128,1536]{1,2,0:T(8,128)(2,1)} %bitcast.163, s32[1024]{0:T(1024)S(1)} %pad_clamp_fusion.9), kind=kCustom, calls=%fused_computation.1.clone.clone.1 | custom fusion | bytes 6291488 | tf_op jit(solution)/shard_map/while/body/eval_jaxpr/jit(_take)/gather | solution.py:50
  204.1 3.3 fusion.83
  207.4 3.7 %fusion.40 = bf16[4,16,1,128,128]{3,4,1,2,0:T(8,128)(2,1)} fusion(s32[]{:T(128)S(6)} %select_n.231, bf16[4,16,1,128,128]{3,4,1,2,0:T(8,128)(2,1)} %collective-permute-done.15), kind=kLoop, calls=%fused_computation.78 | loop fusion | flops 1048576 | bytes 4194308 | tf_op jit(solution)/shard_map/concatenate | solution.py:68
  214.7 3.4 broadcast.166.clone.1
  218.1 34.4 %while.46 = (s32[]{:T(128)}, f32[2,4,128,1536]{3,2,1,0:T(8,128)}, bf16[2,4,2,128,128]{4,3,2,1,0:T(8,128)(2,1)}, s32[2,4,2]{1,0,2:T(2,128)S(1)}, f32[16,12]{1,0:T(8,128)S(1)}, /*index=5*/f32[16,128,128]{1,2,0:T(8,128)}, s32[]{:T(128)}) while((s32[]{:T(128)}, f32[2,4,128,1536]{3,2,1,0:T(8,128)}, ...), condition=%wide.region_5.7_spmd.clone, body=%wide.region_4.6_spmd.clone.sunk | while | flops 410518592 | bytes 26482896 | solution.py:53
  218.3 4.9 %multiply_convert_fusion.10 = bf16[16,128,128,12]{1,2,3,0:T(8,128)(2,1)} fusion(f32[16,12]{1,0:T(8,128)S(1)} %get-tuple-element.491, f32[16,128,128]{1,2,0:T(8,128)} %get-tuple-element.492), kind=kLoop, calls=%fused_computation.36.clone.1 | loop fusion | flops 6291456 | bytes 7340800 | tf_op jit(solution)/shard_map/convert_element_type | solution.py:36
  223.2 5.4 %gather_fusion.2 = bf16[8,128,1536]{1,2,0:T(8,128)(2,1)} fusion(bf16[16,128,1536]{1,2,0:T(8,128)(2,1)} %bitcast.164, s32[1024]{0:T(1024)S(1)} %pad_clamp_fusion.10), kind=kCustom, calls=%fused_computation.2.clone.clone.1 | custom fusion | bytes 6291488 | tf_op jit(solution)/shard_map/while/body/eval_jaxpr/jit(_take)/gather | solution.py:50
  231.9 3.4 fusion.86
  235.5 4.9 %multiply_convert_fusion.10 = bf16[16,128,128,12]{1,2,3,0:T(8,128)(2,1)} fusion(f32[16,12]{1,0:T(8,128)S(1)} %get-tuple-element.491, f32[16,128,128]{1,2,0:T(8,128)} %get-tuple-element.492), kind=kLoop, calls=%fused_computation.36.clone.1 | loop fusion | flops 6291456 | bytes 7340800 | tf_op jit(solution)/shard_map/convert_element_type | solution.py:36
  240.4 5.4 %gather_fusion.2 = bf16[8,128,1536]{1,2,0:T(8,128)(2,1)} fusion(bf16[16,128,1536]{1,2,0:T(8,128)(2,1)} %bitcast.164, s32[1024]{0:T(1024)S(1)} %pad_clamp_fusion.10), kind=kCustom, calls=%fused_computation.2.clone.clone.1 | custom fusion | bytes 6291488 | tf_op jit(solution)/shard_map/while/body/eval_jaxpr/jit(_take)/gather | solution.py:50
  249.1 3.4 fusion.86
  254.7 3.4 broadcast.166.clone
  258.1 34.2 %while.47 = (s32[]{:T(128)}, f32[2,4,128,1536]{3,2,1,0:T(8,128)}, bf16[2,4,2,128,128]{4,3,2,1,0:T(8,128)(2,1)}, s32[2,4,2]{1,0,2:T(2,128)S(1)}, f32[16,12]{1,0:T(8,128)S(1)}, /*index=5*/f32[16,128,128]{1,2,0:T(8,128)}, s32[]{:T(128)}) while((s32[]{:T(128)}, f32[2,4,128,1536]{3,2,1,0:T(8,128)}, ...), condition=%wide.region_7.9_spmd.clone, body=%wide.region_6.8_spmd.clone.sunk | while | flops 410518592 | bytes 26482896 | solution.py:53
  258.3 4.9 %multiply_convert_fusion.11 = bf16[16,128,128,12]{1,2,3,0:T(8,128)(2,1)} fusion(f32[16,12]{1,0:T(8,128)S(1)} %get-tuple-element.470, f32[16,128,128]{1,2,0:T(8,128)} %get-tuple-element.471), kind=kLoop, calls=%fused_computation.50.clone.1 | loop fusion | flops 6291456 | bytes 7340800 | tf_op jit(solution)/shard_map/convert_element_type | solution.py:36
  263.2 5.4 %gather_fusion.3 = bf16[8,128,1536]{1,2,0:T(8,128)(2,1)} fusion(bf16[16,128,1536]{1,2,0:T(8,128)(2,1)} %bitcast.165, s32[1024]{0:T(1024)S(1)} %pad_clamp_fusion.11), kind=kCustom, calls=%fused_computation.3.clone.clone.1 | custom fusion | bytes 6291488 | tf_op jit(solution)/shard_map/while/body/eval_jaxpr/jit(_take)/gather | solution.py:50
  275.4 4.9 %multiply_convert_fusion.11 = bf16[16,128,128,12]{1,2,3,0:T(8,128)(2,1)} fusion(f32[16,12]{1,0:T(8,128)S(1)} %get-tuple-element.470, f32[16,128,128]{1,2,0:T(8,128)} %get-tuple-element.471), kind=kLoop, calls=%fused_computation.50.clone.1 | loop fusion | flops 6291456 | bytes 7340800 | tf_op jit(solution)/shard_map/convert_element_type | solution.py:36
  280.3 5.4 %gather_fusion.3 = bf16[8,128,1536]{1,2,0:T(8,128)(2,1)} fusion(bf16[16,128,1536]{1,2,0:T(8,128)(2,1)} %bitcast.165, s32[1024]{0:T(1024)S(1)} %pad_clamp_fusion.11), kind=kCustom, calls=%fused_computation.3.clone.clone.1 | custom fusion | bytes 6291488 | tf_op jit(solution)/shard_map/while/body/eval_jaxpr/jit(_take)/gather | solution.py:50
  289.0 3.4 fusion.89
  292.3 13.8 %add_add_fusion = f32[2,4,128,1536]{3,2,1,0:T(8,128)} fusion(f32[2,4,128,1536]{3,2,1,0:T(8,128)} %get-tuple-element.117, f32[2,4,128,1536]{3,2,1,0:T(8,128)} %get-tuple-element.116, f32[2,4,128,1536]{3,2,1,0:T(8,128)} %get-tuple-element.114, f32[2,4,128,1536]{3,2,1,0:T(8,128)} %get-tuple-element.115), kind=kLoop, calls=%fused_computation.64 | loop fusion | flops 4718592 | bytes 31457280 | tf_op jit(solution)/shard_map/add | solution.py:122
  306.2 23.5 %all-gather.2.cloned.1.call-done = f32[2,1024,1536]{2,1,0:T(8,128)} async-done(((f32[1,1024,1536]{2,1,0:T(8,128)}), f32[2,1024,1536]{2,1,0:T(8,128)}) %all-gather.2.cloned.1.call-update) | async-done | bytes 12582928 | tf_op jit(solution)/shard_map/all_gather | solution.py:12
  329.6 6.6 %reduce_sum.9 = bf16[1024,1536]{1,0:T(8,128)(2,1)S(1)} reduce(f32[2,1024,1536]{2,1,0:T(8,128)} %all-gather.2.cloned.1.call-done, f32[]{:T(128)} %constant.192.clone.1), dimensions={0}, to_apply=%region_8.10 | reduce | flops 1572864 | bytes 15728644 | tf_op jit(solution)/shard_map/reduce_sum | solution.py:12
  (172 shorter events, 86.9 us)
Async XLA Ops:
  6.5 6.3 %copy-start.1 = (s32[4,1,1,1,16]{4,3,2,1,0:T(1,128)S(1)}, s32[4,1,1,1,16]{4,3,2,1,0:T(1,128)}, u32[]{:S(2)}) copy-start(s32[4,1,1,1,16]{4,3,2,1,0:T(1,128)} %param.21) | copy-start | bytes 772
  6.5 6.3 %copy-start.2 = (s32[4,1,1,1,16,1]{4,5,3,2,1,0:T(1,128)S(1)}, s32[4,1,1,1,16,1]{4,5,3,2,1,0:T(1,128)}, u32[]{:S(2)}) copy-start(s32[4,1,1,1,16,1]{4,5,3,2,1,0:T(1,128)} %param.20) | copy-start | bytes 772
  6.5 8.3 %copy-start.4 = (s32[1,1,8]{2,1,0:T(1,128)S(1)}, s32[1,1,8]{2,1,0:T(1,128)}, u32[]{:S(2)}) copy-start(s32[1,1,8]{2,1,0:T(1,128)} %param.18) | copy-start | bytes 100
  6.5 12.8 %copy-start = (bf16[1,1,8,2,128,128]{5,4,3,2,1,0:T(8,128)(2,1)S(1)}, bf16[1,1,8,2,128,128]{5,4,3,2,1,0:T(8,128)(2,1)}, u32[]{:S(2)}) copy-start(bf16[1,1,8,2,128,128]{5,4,3,2,1,0:T(8,128)(2,1)} %param.16) | copy-start | bytes 1572868
  6.5 14.1 %copy-start.3 = (s32[1,1,8,2]{2,3,1,0:T(2,128)S(1)}, s32[1,1,8,2]{2,3,1,0:T(2,128)}, u32[]{:S(2)}) copy-start(s32[1,1,8,2]{2,3,1,0:T(2,128)} %param.17) | copy-start | bytes 196
  6.5 323.1 %all-gather.2.cloned.1.call-start = ((), (), s32[]{:S(2)}) async-start(), calls=%async_computation | async-start | bytes 18874368 | tf_op jit(solution)/shard_map/all_gather | solution.py:12
  9.7 105.4 %collective-permute-start.3 = (bf16[4,16,1,128,128]{3,4,1,2,0:T(8,128)(2,1)S(1)}, bf16[4,16,1,128,128]{3,4,1,2,0:T(8,128)(2,1)}, u32[]{:S(2)}, u32[]{:S(2)}) collective-permute-start(bf16[4,16,1,128,128]{3,4,1,2,0:T(8,128)(2,1)S(1)} %bitcast.171), channel_id=1, source_target_pairs={{0,16},{16,0},{1,17},{17,1},{2,18},{18,2},{3,19},{19,3},{4,20},{20... | collective-permute-start | bytes 6291464 | tf_op jit(solution)/shard_map/ppermute | solution.py:23
  12.8 53.9 %collective-permute-start.5 = (s32[4,16]{1,0:T(4,128)S(1)}, s32[4,16]{1,0:T(4,128)S(1)}, u32[]{:S(2)}, u32[]{:S(2)}) collective-permute-start(s32[4,16]{1,0:T(4,128)S(1)} %bitcast.185), channel_id=1, source_target_pairs={{0,16},{16,0},{1,17},{17,1},{2,18},{18,2},{3,19},{19,3},{4,20},{20... | collective-permute-start | bytes 776 | tf_op jit(solution)/shard_map/ppermute | solution.py:23
  12.9 54.5 %collective-permute-start.4 = (s32[4,16,1]{1,0,2:T(4,128)S(1)}, s32[4,16,1]{1,0,2:T(4,128)S(1)}, u32[]{:S(2)}, u32[]{:S(2)}) collective-permute-start(s32[4,16,1]{1,0,2:T(4,128)S(1)} %bitcast.187), channel_id=1, source_target_pairs={{0,16},{16,0},{1,17},{17,1},{2,18},{18,2},{3,19},{19,3},{4,20},{20... | collective-permute-start | bytes 776 | tf_op jit(solution)/shard_map/ppermute | solution.py:23
  14.8 5.8 %collective-permute-start = (s32[8]{0:T(128)S(1)}, s32[8]{0:T(128)S(1)}, u32[]{:S(2)}, u32[]{:S(2)}) collective-permute-start(s32[8]{0:T(128)S(1)} %bitcast.190), channel_id=1, source_target_pairs={{0,14},{2,0},{4,2},{6,4},{8,6},{10,8},{12,10},{14,12},{1,15},{3,1}... | collective-permute-start | bytes 104 | tf_op jit(solution)/shard_map/ppermute | solution.py:23
  19.4 58.5 %collective-permute-start.1 = (bf16[8,2,128,128]{3,2,1,0:T(8,128)(2,1)S(1)}, bf16[8,2,128,128]{3,2,1,0:T(8,128)(2,1)S(1)}, u32[]{:S(2)}, u32[]{:S(2)}) collective-permute-start(bf16[8,2,128,128]{3,2,1,0:T(8,128)(2,1)S(1)} %bitcast.176), channel_id=1, source_target_pairs={{0,14},{2,0},{4,2},{6,4},{8,6},{10,8},{12,10},{14,12},{1,15},{3,1}... | collective-permute-start | bytes 1572872 | tf_op jit(solution)/shard_map/ppermute | solution.py:23
  20.7 11.3 %collective-permute-start.2 = (s32[8,2]{0,1:T(2,128)S(1)}, s32[8,2]{0,1:T(2,128)S(1)}, u32[]{:S(2)}, u32[]{:S(2)}) collective-permute-start(s32[8,2]{0,1:T(2,128)S(1)} %bitcast.189), channel_id=1, source_target_pairs={{0,14},{2,0},{4,2},{6,4},{8,6},{10,8},{12,10},{14,12},{1,15},{3,1}... | collective-permute-start | bytes 200 | tf_op jit(solution)/shard_map/ppermute | solution.py:23
  32.0 4.5 %collective-permute-start.6 = (s32[8]{0:T(128)S(1)}, s32[8]{0:T(128)S(1)}, u32[]{:S(2)}, u32[]{:S(2)}) collective-permute-start(s32[8]{0:T(128)S(1)} %broadcast_select_fusion.6), channel_id=1, source_target_pairs={{0,14},{2,0},{4,2},{6,4},{8,6},{10,8},{12,10},{14,12},{1,15},{3,1}... | collective-permute-start | bytes 104 | tf_op jit(solution)/shard_map/ppermute | solution.py:23
  36.6 6.3 %collective-permute-start.12 = (s32[8]{0:T(128)S(1)}, s32[8]{0:T(128)S(1)}, u32[]{:S(2)}, u32[]{:S(2)}) collective-permute-start(s32[8]{0:T(128)S(1)} %collective-permute-done.6), channel_id=1, source_target_pairs={{0,14},{2,0},{4,2},{6,4},{8,6},{10,8},{12,10},{14,12},{1,15},{3,1}... | collective-permute-start | bytes 104 | tf_op jit(solution)/shard_map/ppermute | solution.py:23
  42.8 6.3 %collective-permute-start.8 = (s32[8,2]{0,1:T(2,128)S(1)}, s32[8,2]{0,1:T(2,128)S(1)}, u32[]{:S(2)}, u32[]{:S(2)}) collective-permute-start(s32[8,2]{0,1:T(2,128)S(1)} %broadcast_select_fusion.5), channel_id=1, source_target_pairs={{0,14},{2,0},{4,2},{6,4},{8,6},{10,8},{12,10},{14,12},{1,15},{3,1}... | collective-permute-start | bytes 200 | tf_op jit(solution)/shard_map/ppermute | solution.py:23
  49.1 6.3 %collective-permute-start.18 = (s32[8]{0:T(128)S(1)}, s32[8]{0:T(128)S(1)}, u32[]{:S(2)}, u32[]{:S(2)}) collective-permute-start(s32[8]{0:T(128)S(1)} %collective-permute-done.12), channel_id=1, source_target_pairs={{0,14},{2,0},{4,2},{6,4},{8,6},{10,8},{12,10},{14,12},{1,15},{3,1}... | collective-permute-start | bytes 104 | tf_op jit(solution)/shard_map/ppermute | solution.py:23
  55.4 6.3 %collective-permute-start.14 = (s32[8,2]{0,1:T(2,128)S(1)}, s32[8,2]{0,1:T(2,128)S(1)}, u32[]{:S(2)}, u32[]{:S(2)}) collective-permute-start(s32[8,2]{0,1:T(2,128)S(1)} %collective-permute-done.8), channel_id=1, source_target_pairs={{0,14},{2,0},{4,2},{6,4},{8,6},{10,8},{12,10},{14,12},{1,15},{3,1}... | collective-permute-start | bytes 200 | tf_op jit(solution)/shard_map/ppermute | solution.py:23
  61.7 7.4 %collective-permute-start.20 = (s32[8,2]{0,1:T(2,128)S(1)}, s32[8,2]{0,1:T(2,128)S(1)}, u32[]{:S(2)}, u32[]{:S(2)}) collective-permute-start(s32[8,2]{0,1:T(2,128)S(1)} %collective-permute-done.14), channel_id=1, source_target_pairs={{0,14},{2,0},{4,2},{6,4},{8,6},{10,8},{12,10},{14,12},{1,15},{3,1}... | collective-permute-start | bytes 200 | tf_op jit(solution)/shard_map/ppermute | solution.py:23
  66.8 3.7 %collective-permute-start.11 = (s32[4,16]{1,0:T(4,128)S(1)}, s32[4,16]{1,0:T(4,128)S(1)}, u32[]{:S(2)}, u32[]{:S(2)}) collective-permute-start(s32[4,16]{1,0:T(4,128)S(1)} %fusion.65), channel_id=1, source_target_pairs={{0,16},{16,0},{1,17},{17,1},{2,18},{18,2},{3,19},{19,3},{4,20},{20... | collective-permute-start | bytes 776 | tf_op jit(solution)/shard_map/ppermute | solution.py:23
  67.5 3.7 %collective-permute-start.10 = (s32[4,16,1]{1,0,2:T(4,128)S(1)}, s32[4,16,1]{1,0,2:T(4,128)S(1)}, u32[]{:S(2)}, u32[]{:S(2)}) collective-permute-start(s32[4,16,1]{1,0,2:T(4,128)S(1)} %fusion.62), channel_id=1, source_target_pairs={{0,16},{16,0},{1,17},{17,1},{2,18},{18,2},{3,19},{19,3},{4,20},{20... | collective-permute-start | bytes 776 | tf_op jit(solution)/shard_map/ppermute | solution.py:23
  70.5 3.7 %collective-permute-start.17 = (s32[4,16]{1,0:T(4,128)S(1)}, s32[4,16]{1,0:T(4,128)S(1)}, u32[]{:S(2)}, u32[]{:S(2)}) collective-permute-start(s32[4,16]{1,0:T(4,128)S(1)} %constant_dynamic-slice_fusion.8), channel_id=1, source_target_pairs={{0,16},{16,0},{1,17},{17,1},{2,18},{18,2},{3,19},{19,3},{4,20},{20... | collective-permute-start | bytes 776 | tf_op jit(solution)/shard_map/ppermute | solution.py:23
  71.2 3.7 %collective-permute-start.16 = (s32[4,16,1]{1,0,2:T(4,128)S(1)}, s32[4,16,1]{1,0,2:T(4,128)S(1)}, u32[]{:S(2)}, u32[]{:S(2)}) collective-permute-start(s32[4,16,1]{1,0,2:T(4,128)S(1)} %constant_dynamic-slice_fusion.9), channel_id=1, source_target_pairs={{0,16},{16,0},{1,17},{17,1},{2,18},{18,2},{3,19},{19,3},{4,20},{20... | collective-permute-start | bytes 776 | tf_op jit(solution)/shard_map/ppermute | solution.py:23
  74.2 3.7 %collective-permute-start.23 = (s32[4,16]{1,0:T(4,128)S(1)}, s32[4,16]{1,0:T(4,128)S(1)}, u32[]{:S(2)}, u32[]{:S(2)}) collective-permute-start(s32[4,16]{1,0:T(4,128)S(1)} %constant_dynamic-slice_fusion.6), channel_id=1, source_target_pairs={{0,16},{16,0},{1,17},{17,1},{2,18},{18,2},{3,19},{19,3},{4,20},{20... | collective-permute-start | bytes 776 | tf_op jit(solution)/shard_map/ppermute | solution.py:23
  74.8 6.5 %collective-permute-start.22 = (s32[4,16,1]{1,0,2:T(4,128)S(1)}, s32[4,16,1]{1,0,2:T(4,128)S(1)}, u32[]{:S(2)}, u32[]{:S(2)}) collective-permute-start(s32[4,16,1]{1,0,2:T(4,128)S(1)} %constant_dynamic-slice_fusion.7), channel_id=1, source_target_pairs={{0,16},{16,0},{1,17},{17,1},{2,18},{18,2},{3,19},{19,3},{4,20},{20... | collective-permute-start | bytes 776 | tf_op jit(solution)/shard_map/ppermute | solution.py:23
  78.7 14.3 %collective-permute-start.7 = (bf16[8,2,128,128]{3,2,1,0:T(8,128)(2,1)S(1)}, bf16[8,2,128,128]{3,2,1,0:T(8,128)(2,1)S(1)}, u32[]{:S(2)}, u32[]{:S(2)}) collective-permute-start(bf16[8,2,128,128]{3,2,1,0:T(8,128)(2,1)S(1)} %get-tuple-element.303), channel_id=1, source_target_pairs={{0,14},{2,0},{4,2},{6,4},{8,6},{10,8},{12,10},{14,12},{1,15},{3,1}... | collective-permute-start | bytes 1572872 | tf_op jit(solution)/shard_map/ppermute | solution.py:23
  93.0 16.0 %collective-permute-start.13 = (bf16[8,2,128,128]{3,2,1,0:T(8,128)(2,1)S(1)}, bf16[8,2,128,128]{3,2,1,0:T(8,128)(2,1)S(1)}, u32[]{:S(2)}, u32[]{:S(2)}) collective-permute-start(bf16[8,2,128,128]{3,2,1,0:T(8,128)(2,1)S(1)} %collective-permute-done.7), channel_id=1, source_target_pairs={{0,14},{2,0},{4,2},{6,4},{8,6},{10,8},{12,10},{14,12},{1,15},{3,1}... | collective-permute-start | bytes 1572872 | tf_op jit(solution)/shard_map/ppermute | solution.py:23
  109.0 15.1 %collective-permute-start.19 = (bf16[8,2,128,128]{3,2,1,0:T(8,128)(2,1)S(1)}, bf16[8,2,128,128]{3,2,1,0:T(8,128)(2,1)S(1)}, u32[]{:S(2)}, u32[]{:S(2)}) collective-permute-start(bf16[8,2,128,128]{3,2,1,0:T(8,128)(2,1)S(1)} %collective-permute-done.13), channel_id=1, source_target_pairs={{0,14},{2,0},{4,2},{6,4},{8,6},{10,8},{12,10},{14,12},{1,15},{3,1}... | collective-permute-start | bytes 1572872 | tf_op jit(solution)/shard_map/ppermute | solution.py:23
  120.6 42.5 %collective-permute-start.9 = (bf16[4,16,1,128,128]{3,4,1,2,0:T(8,128)(2,1)}, bf16[4,16,1,128,128]{3,4,1,2,0:T(8,128)(2,1)}, u32[]{:S(2)}, u32[]{:S(2)}) collective-permute-start(bf16[4,16,1,128,128]{3,4,1,2,0:T(8,128)(2,1)} %fusion.43), channel_id=1, source_target_pairs={{0,16},{16,0},{1,17},{17,1},{2,18},{18,2},{3,19},{19,3},{4,20},{20... | collective-permute-start | bytes 6291464 | tf_op jit(solution)/shard_map/ppermute | solution.py:23
  169.0 38.5 %collective-permute-start.15 = (bf16[4,16,1,128,128]{3,4,1,2,0:T(8,128)(2,1)}, bf16[4,16,1,128,128]{3,4,1,2,0:T(8,128)(2,1)}, u32[]{:S(2)}, u32[]{:S(2)}) collective-permute-start(bf16[4,16,1,128,128]{3,4,1,2,0:T(8,128)(2,1)} %fusion.41), channel_id=1, source_target_pairs={{0,16},{16,0},{1,17},{17,1},{2,18},{18,2},{3,19},{19,3},{4,20},{20... | collective-permute-start | bytes 6291464 | tf_op jit(solution)/shard_map/ppermute | solution.py:23
  213.2 39.2 %collective-permute-start.21 = (bf16[4,16,1,128,128]{3,4,1,2,0:T(8,128)(2,1)}, bf16[4,16,1,128,128]{3,4,1,2,0:T(8,128)(2,1)}, u32[]{:S(2)}, u32[]{:S(2)}) collective-permute-start(bf16[4,16,1,128,128]{3,4,1,2,0:T(8,128)(2,1)} %fusion.40), channel_id=1, source_target_pairs={{0,16},{16,0},{1,17},{17,1},{2,18},{18,2},{3,19},{19,3},{4,20},{20... | collective-permute-start | bytes 6291464 | tf_op jit(solution)/shard_map/ppermute | solution.py:23
Sparse Core Ops, SparseCore 0:
  306.3 23.2 all-gather.1
